TPU v7x, 256 devices: a whole 4x4x8 slice. The times are simulated.
256 devices in a mesh: section: 2 (over core), tile: 128 (over y, x, z).
Axes of the slice: x: 4, y: 4, z: 8, core: 2. Of those that a mesh axis runs over, the one named last changes fastest.
Arguments:
- aerial_patch_grid: bfloat16 [384, 384, 768], P('tile'), may hold values from -6 to 6
- patch_conv_weight: bfloat16 [3, 4, 4, 96], replicated, may hold values from -0.875 to 0.875
- patch_bias: float32 [96], replicated, may hold values from -3 to 3
- merging_conv_weight: bfloat16 [2, 2, 96, 192], replicated, may hold values from -0.3125 to 0.3125
- merge_bias: float32 [192], replicated, may hold values from -3 to 3
- down_weight: bfloat16 [3, 3, 192, 384], replicated, may hold values from -0.15625 to 0.15625
- down_bias: float32 [384], replicated, may hold values from -3 to 3
- norm_gain: float32 [384], replicated, may hold values from 0.1 to 1.9
- spectral_filter: bfloat16 [384, 2, 384, 384], P('tile'), may hold values from -6 to 6
Outputs:
- block_output: bfloat16 [384, 384, 384], P('section', 'tile')
All inputs are finite; a program needn't handle non-finite values.
Results may differ from a plain program's by a relative error of at most 0.015.
Values may be sent and summed in bfloat16 or wider, within the bound.
A program may use at most 64 MiB of HBM per device.

v0:
```python
import math
import jax
import jax.numpy as jnp
from jax import lax
from jax.sharding import PartitionSpec as P

EPSILON = 1e-05


def from_behind(block, axis, distance):
    devices = range(lax.axis_size(axis))
    route = [(i - distance, i) for i in devices if i - distance in devices]
    return lax.ppermute(block, axis, route)


def fourier_tables(length):
    indices = jnp.arange(length, dtype=jnp.int32)
    product = indices[:, None] * indices[None, :] % length
    angles = product.astype(jnp.float32) * (2.0 * math.pi / length)
    return (jnp.cos(angles).astype(jnp.bfloat16), jnp.sin(angles).astype(jnp.bfloat16))


def one_hot_rows(indices, width):
    return (indices[:, None] == jnp.arange(width, dtype=jnp.int32)[None, :]).astype(jnp.bfloat16)


def spread_kernel(weight_rows, row_pick, row_cell, col_cell, width, out_cols):
    picked = jnp.dot(
        one_hot_rows(row_pick, weight_rows.shape[0]),
        weight_rows,
        preferred_element_type=jnp.float32,
    ).astype(jnp.bfloat16)
    col = jnp.arange(out_cols, dtype=jnp.int32)
    repeat = one_hot_rows(col % width, width).T
    full = jnp.dot(picked, repeat, preferred_element_type=jnp.float32)
    mask = row_cell[:, None] == col_cell[None, :]
    return jnp.where(mask, full, 0.0).astype(jnp.bfloat16)


def patch_kernel_matrix(patch_conv_weight):
    band_count = patch_conv_weight.shape[0]
    width = patch_conv_weight.shape[3]
    row = jnp.arange(band_count * 256, dtype=jnp.int32)
    pick = row // 256 * 16 + row // 16 % 4 * 4 + row % 4
    row_cell = row // 64 % 4 * 4 + row // 4 % 4
    col = jnp.arange(16 * width, dtype=jnp.int32)
    col_cell = col // width
    weight_rows = patch_conv_weight.reshape(band_count * 16, width)
    return spread_kernel(weight_rows, pick, row_cell, col_cell, width, 16 * width)


def merging_kernel_matrix(merging_conv_weight):
    in_width = merging_conv_weight.shape[2]
    out_width = merging_conv_weight.shape[3]
    row = jnp.arange(16 * in_width, dtype=jnp.int32)
    pos = row // in_width
    pick = (pos // 4 % 2 * 2 + pos % 2) * in_width + row % in_width
    row_cell = pos // 8 * 2 + pos // 2 % 2
    col = jnp.arange(4 * out_width, dtype=jnp.int32)
    col_cell = col // out_width
    weight_rows = merging_conv_weight.reshape(4 * in_width, out_width)
    return spread_kernel(weight_rows, pick, row_cell, col_cell, out_width, 4 * out_width)


def down_matrices(down_weight):
    nothing = jnp.zeros_like(down_weight[0, 0])
    in_width = down_weight.shape[2]
    out_width = down_weight.shape[3]

    def arrange(entries):
        return jnp.stack(
            [jnp.stack(entries[0], axis=0), jnp.stack(entries[1], axis=0)], axis=0
        ).reshape(4 * in_width, out_width)

    own_taps = arrange(
        [[down_weight[1, 1], down_weight[1, 2]], [down_weight[2, 1], down_weight[2, 2]]]
    )
    upper_taps = arrange([[nothing, nothing], [down_weight[0, 1], down_weight[0, 2]]])
    left_taps = arrange([[nothing, down_weight[1, 0]], [nothing, down_weight[2, 0]]])
    corner_taps = arrange([[nothing, nothing], [nothing, down_weight[0, 0]]])
    return (own_taps, upper_taps, left_taps, corner_taps)


def stem_layers(aerial_patch_grid, patch_conv_weight, patch_bias, merging_conv_weight, merge_bias):
    initial_layer = jnp.einsum(
        "zji,if->zjf",
        aerial_patch_grid,
        patch_kernel_matrix(patch_conv_weight),
        preferred_element_type=jnp.float32,
    )
    initial_layer = jax.nn.gelu(initial_layer + jnp.tile(patch_bias, 16), approximate=True).astype(
        jnp.bfloat16
    )
    layer_two = jnp.einsum(
        "zji,if->zjf",
        initial_layer,
        merging_kernel_matrix(merging_conv_weight),
        preferred_element_type=jnp.float32,
    )
    return jax.nn.gelu(layer_two + jnp.tile(merge_bias, 4), approximate=True).astype(jnp.bfloat16)


def rim_above(extended):
    return from_behind(extended[-1:], "tile", 1)


def down_conv(upper_rim, extended, down_weight, down_bias):
    stacked = jnp.concatenate([upper_rim, extended], axis=0)
    own_taps, upper_taps, left_taps, corner_taps = down_matrices(down_weight)
    summed = jnp.einsum(
        "rwk,kc->crw", stacked[1:, 1:], own_taps, preferred_element_type=jnp.float32
    )
    summed = summed + jnp.einsum(
        "rwk,kc->crw", stacked[:-1, 1:], upper_taps, preferred_element_type=jnp.float32
    )
    summed = summed + jnp.einsum(
        "rwk,kc->crw", stacked[1:, :-1], left_taps, preferred_element_type=jnp.float32
    )
    summed = summed + jnp.einsum(
        "rwk,kc->crw", stacked[:-1, :-1], corner_taps, preferred_element_type=jnp.float32
    )
    return (summed + down_bias[:, None, None]).astype(jnp.bfloat16)


def layer_norm(features, norm_gain):
    values = features.astype(jnp.float32)
    mean_value = jnp.mean(values, axis=0, keepdims=True)
    centered = values - mean_value
    variance = jnp.mean(centered * centered, axis=0, keepdims=True)
    return (norm_gain[:, None, None] * centered * lax.rsqrt(variance + EPSILON)).astype(
        jnp.bfloat16
    )


def filter_columns(row_spectrum, kernel, forward_h, inverse_h):
    spectrum = jnp.einsum(
        "puqh,chqw->cpuw", forward_h, row_spectrum, preferred_element_type=jnp.float32
    ).astype(jnp.bfloat16)
    spec_real = spectrum[:, 0].astype(jnp.float32)
    spec_imag = spectrum[:, 1].astype(jnp.float32)
    filter_real = kernel[:, 0].astype(jnp.float32)
    filter_imag = kernel[:, 1].astype(jnp.float32)
    weighted = jnp.stack(
        [
            filter_real * spec_real - filter_imag * spec_imag,
            filter_real * spec_imag + filter_imag * spec_real,
        ],
        axis=1,
    ).astype(jnp.bfloat16)
    return jnp.einsum(
        "qhpu,cpuw->chqw", inverse_h, weighted, preferred_element_type=jnp.float32
    ).astype(jnp.bfloat16)


def local(
    aerial_patch_grid,
    patch_conv_weight,
    patch_bias,
    merging_conv_weight,
    merge_bias,
    down_weight,
    down_bias,
    norm_gain,
    spectral_filter,
):
    section_index = lax.axis_index("section")
    field_cols = aerial_patch_grid.shape[1]
    channels = down_weight.shape[3]
    full_rows = spectral_filter.shape[2]
    half_channels = channels // 2
    cell_half = field_cols // 2
    image_part = lax.dynamic_slice_in_dim(
        aerial_patch_grid, section_index * cell_half, cell_half, 1
    )
    layer_two = stem_layers(
        image_part, patch_conv_weight, patch_bias, merging_conv_weight, merge_bias
    )
    left_column = from_behind(layer_two[:, -1:], "section", 1)
    extended = jnp.concatenate([left_column, layer_two], axis=1)
    upper_rim = rim_above(extended)
    feature_half = down_conv(upper_rim, extended, down_weight, down_bias)
    normed_half = layer_norm(feature_half, norm_gain)
    fields = lax.all_to_all(normed_half, "tile", split_axis=0, concat_axis=1, tiled=True)
    fields = lax.all_gather(fields, "section", axis=2, tiled=True)
    cos_h, sin_h = fourier_tables(full_rows)
    if full_rows == field_cols:
        cos_w, sin_w = (cos_h, sin_h)
    else:
        cos_w, sin_w = fourier_tables(field_cols)
    cos_part = lax.dynamic_slice_in_dim(cos_w, section_index * cell_half, cell_half, 1)
    sin_part = lax.dynamic_slice_in_dim(sin_w, section_index * cell_half, cell_half, 1)
    forward_table = jnp.stack([cos_part, -sin_part], axis=1)
    inverse_table = jnp.stack([cos_part, -sin_part], axis=0)
    forward_h = jnp.stack(
        [jnp.stack([cos_h, sin_h], axis=1), jnp.stack([-sin_h, cos_h], axis=1)], axis=0
    )
    inverse_h = jnp.stack(
        [jnp.stack([cos_h, -sin_h], axis=1), jnp.stack([sin_h, cos_h], axis=1)], axis=0
    )
    norm_scale = 1.0 / (full_rows * field_cols)
    kernel_part = lax.dynamic_slice_in_dim(spectral_filter, section_index * cell_half, cell_half, 3)
    frequency_rows = jnp.einsum(
        "chx,xqw->chqw", fields, forward_table, preferred_element_type=jnp.float32
    ).astype(jnp.bfloat16)
    back_rows = filter_columns(frequency_rows, kernel_part, forward_h, inverse_h)
    back_rows = lax.all_gather(back_rows, "section", axis=3, tiled=True)
    result = jnp.einsum(
        "chqw,qwv->chv", back_rows, inverse_table, preferred_element_type=jnp.float32
    )
    filtered_fields = (result * norm_scale).astype(jnp.bfloat16)
    rows_back = lax.all_to_all(filtered_fields, "tile", split_axis=1, concat_axis=0, tiled=True)
    summed = (feature_half.astype(jnp.float32) + rows_back.astype(jnp.float32)).astype(jnp.bfloat16)
    kept = lax.dynamic_slice_in_dim(summed, section_index * half_channels, half_channels, 0)
    sent = lax.dynamic_slice_in_dim(summed, (1 - section_index) * half_channels, half_channels, 0)
    received = lax.ppermute(sent, "section", [(0, 1), (1, 0)])
    return jnp.where(
        section_index == 0,
        jnp.concatenate([kept, received], axis=2),
        jnp.concatenate([received, kept], axis=2),
    )


def solution(mesh):
    return jax.shard_map(
        local,
        mesh=mesh,
        in_specs=(
            P("tile", None, None),
            P(),
            P(),
            P(),
            P(),
            P(),
            P(),
            P(),
            P("tile", None, None, None),
        ),
        out_specs=P("section", "tile", None),
        check_vma=False,
    )
```

profile of v0, /device:TPU:1, one launch (start us, length us, event | category | flops | bytes accessed | tf_op | source)
XLA Modules:
  0.0 175.3 jit_solution(6050538914939704282)
XLA Ops:
  6.6 0.8 tile.4
  7.4 0.1 add.318
  7.5 0.7 tile.5
  8.2 0.1 add.331
  8.3 2.5 %convolution_convert_fusion = bf16[1536,192]{0,1:T(8,128)(2,1)} fusion(bf16[384,192]{1,0:T(8,128)(2,1)} %bitcast.142, s32[1536]{0:T(1024)S(1)} %fusion.101), kind=kOutput, calls=%fused_computation.14 | convolution fusion | flops 227377152 | bytes 743424 | tf_op jit(solution)/shard_map/dot_general | solution.py:28
  10.8 3.5 %fusion.8 = bf16[768,1536,1]{1,0,2:T(8,128)(2,1)} fusion(s32[1536]{0:T(1024)S(1)} %get-tuple-element.41, s32[768]{0:T(1024)S(1)} %get-tuple-element.42, bf16[48,96]{1,0:T(8,128)(2,1)} %bitcast.143, s32[1536]{0:T(1024)S(1)} %get-tuple-element.40, s32[768]{0:T(1024)S(1)} %get-tuple-element.43), kind=kOutput, calls=%fused_computation.11 | convolution fusion | flops 237367296 | bytes 2386944 | tf_op jit(solution)/shard_map/dot_general | solution.py:35
  14.3 5.0 %fusion.7 = bf16[3,192,1536]{2,1,0:T(8,128)(2,1)} fusion(bf16[768,1536,1]{1,0,2:T(8,128)(2,1)} %fusion.8, f32[1536]{0:T(1024)S(1)} %add.318, bf16[3,384,768]{2,1,0:T(8,128)(2,1)S(1)} %copy-done, s32[]{:T(128)S(6)} %select_n.229), kind=kOutput, calls=%fused_computation.10 | convolution fusion | flops 1367801856 | bytes 5021700 | tf_op jit(solution)/shard_map/zji,if->zjf/dot_general | solution.py:85
  19.3 4.3 %fusion.17 = bf16[3,192,768]{2,1,0:T(8,128)(2,1)S(1)} fusion(bf16[3,192,1536]{2,1,0:T(8,128)(2,1)} %fusion.7, bf16[1536,192]{0,1:T(8,128)(2,1)} %convolution_convert_fusion, s32[768]{0:T(1024)S(1)} %get-tuple-element.45, s32[1536]{0:T(1024)S(1)} %fusion.94, f32[768]{0:T(1024)S(1)} %add.331, s32[768]{0:T(1024)S(1)} %get-tuple-element.44), kind=kOutput, calls=%fused_computation.23 | convolution fusion | flops 1820049408 | bytes 3259392 | tf_op jit(solution)/shard_map/zji,if->zjf/dot_general | solution.py:94
  23.6 1.3 collective-permute-start
  24.9 1.5 slice_bitcast_fusion.2
  26.5 0.1 maximum_bitcast_fusion.6
  26.5 0.9 pad_maximum_fusion.6
  27.5 0.9 pad_maximum_fusion.7
  28.4 0.4 collective-permute-done
  28.8 0.1 pad_maximum_fusion.8
  28.9 4.0 %collective-permute-start.1 = (bf16[1,193,768]{2,1,0:T(8,128)(2,1)S(1)}, bf16[1,193,768]{2,1,0:T(8,128)(2,1)S(1)}, u32[]{:S(2)}, u32[]{:S(2)}) collective-permute-start(bf16[1,193,768]{2,1,0:T(8,128)(2,1)S(1)} %pad_maximum_fusion.8), channel_id=1, source_target_pairs={{0,1},{1,2},{2,3},{3,4},{4,5},{5,6},{6,7},{7,8},{8,9},{9,10},{10,1... | collective-permute-start | bytes 889352 | tf_op jit(solution)/shard_map/ppermute | solution.py:13
  32.9 0.9 stack.117
  33.8 0.9 stack.125
  34.7 1.7 fusion.135
  36.4 1.9 %collective-permute-done.1 = bf16[1,193,768]{2,1,0:T(8,128)(2,1)S(1)} collective-permute-done((bf16[1,193,768]{2,1,0:T(8,128)(2,1)S(1)}, bf16[1,193,768]{2,1,0:T(8,128)(2,1)S(1)}, u32[]{:S(2)}, u32[]{:S(2)}) %collective-permute-start.1) | collective-permute-done | bytes 296480 | tf_op jit(solution)/shard_map/ppermute | solution.py:13
  38.3 0.2 maximum_maximum_fusion
  38.5 0.6 fusion.41
  39.2 0.4 copy-done.1
  39.6 0.6 convolution_add_fusion.1
  40.2 0.1 copy-done.2
  40.3 0.8 convert_reduce_fusion
  41.0 0.4 fusion.35
  41.4 0.2 fusion.34
  41.7 1.4 copy.31
  43.1 17.3 %all-to-all-start = ((bf16[384,3,192]{2,1,0:T(4,128)(2,1)}), bf16[384,3,192]{2,1,0:T(4,128)(2,1)S(1)}, u32[]{:S(2)}, u32[]{:S(2)}) async-start(bf16[384,3,192]{2,1,0:T(4,128)(2,1)} %copy.31), calls=%async_computation | async-start | bytes 1572864 | tf_op jit(solution)/shard_map/all_to_all | solution.py:183
  60.4 2.8 %constant_dynamic-slice_fusion = (bf16[3,1,384,192]{3,2,1,0:T(8,128)(2,1)}, bf16[3,1,384,192]{3,2,1,0:T(8,128)(2,1)}) fusion(bf16[3,2,384,384]{3,2,1,0:T(8,128)(2,1)} %param.17, s32[]{:T(128)S(6)} %select_n.229, s32[]{:T(128)S(6)} %add.349), kind=kLoop, calls=%fused_computation.233 | loop fusion | bytes 1769480 | tf_op jit(solution)/shard_map/slice | solution.py:141
  63.2 2.1 %copy.50 = bf16[3,1,384,192]{2,3,1,0:T(8,128)(2,1)} copy(bf16[3,1,384,192]{3,2,1,0:T(8,128)(2,1)} %get-tuple-element.7) | data formatting | bytes 884736
  65.3 2.1 %copy.51 = bf16[3,1,384,192]{2,3,1,0:T(8,128)(2,1)} copy(bf16[3,1,384,192]{3,2,1,0:T(8,128)(2,1)} %get-tuple-element.8) | data formatting | bytes 884736
  67.4 0.4 fusion.56
  67.7 1.6 fusion.79
  69.3 1.6 fusion.80
  71.0 2.3 %fusion.77 = bf16[384,1,384]{2,0,1:T(8,128)(2,1)S(1)} fusion(), kind=kLoop, calls=%fused_computation.132 | loop fusion | flops 1916928 | bytes 294912 | tf_op jit(solution)/shard_map/neg | solution.py:195
  73.3 2.6 %sine_convert_fusion = (bf16[384,1,384]{2,0,1:T(8,128)(2,1)S(1)}, bf16[384,1,384]{2,0,1:T(8,128)(2,1)S(1)}) fusion(), kind=kLoop, calls=%fused_computation.93 | loop fusion | flops 1622016 | bytes 589824 | tf_op jit(solution)/shard_map/convert_element_type | solution.py:20
  75.9 1.5 fusion.53
  77.4 6.4 %all-to-all-done = bf16[384,3,192]{2,1,0:T(4,128)(2,1)S(1)} async-done(((bf16[384,3,192]{2,1,0:T(4,128)(2,1)}), bf16[384,3,192]{2,1,0:T(4,128)(2,1)S(1)}, u32[]{:S(2)}, u32[]{:S(2)}) %all-to-all-start) | async-done | bytes 442400 | tf_op jit(solution)/shard_map/all_to_all | solution.py:183
  83.8 1.2 copy.33
  85.0 1.5 all_to_all.23
  86.5 0.3 copy.34
  86.8 6.0 %all_gather.6 = bf16[3,384,384]{1,2,0:T(8,128)(2,1)} all-gather(bf16[3,384,192]{1,2,0:T(8,128)(2,1)S(1)} %copy.34), channel_id=1, replica_groups=mesh['section'=2,'tile'=128] {'section'}, dimensions={2}, use_global_device_ids=true | all-gather | bytes 1327104 | tf_op jit(solution)/shard_map/all_gather | solution.py:184
  92.8 4.1 %fusion.21 = bf16[3,2,384,192]{2,3,1,0:T(8,128)(2,1)} fusion(bf16[1,384,2,384]{3,1,2,0:T(8,128)(2,1)} %get-tuple-element.29, bf16[1,384,2,384]{3,1,2,0:T(8,128)(2,1)} %get-tuple-element.22, bf16[3,384,384]{1,2,0:T(8,128)(2,1)} %all_gather.6, bf16[384,1,192]{0,2,1:T(8,128)(2,1)} %get-tuple-element.21, bf16[384,1,192]{0,2,1:T(8,128)(2,1)} %get-tuple-element.19), kind=kOutput, calls=%fused_computation.35 | convolution fusion | flops 1023049728 | bytes 3244032 | tf_op jit(solution)/shard_map/puqh,chqw->cpuw/dot_general | solution.py:136
  96.9 1.6 fusion.37
  98.5 1.8 %fusion.22 = bf16[3,384,2,192]{1,3,2,0:T(8,128)(2,1)} fusion(bf16[1,384,2,384]{3,1,2,0:T(8,128)(2,1)S(1)} %copy-done.6, bf16[1,384,2,384]{3,1,2,0:T(8,128)(2,1)S(1)} %copy-done.7, bf16[3,1,384,192]{2,3,1,0:T(8,128)(2,1)S(1)} %get-tuple-element.6, bf16[3,1,384,192]{2,3,1,0:T(8,128)(2,1)S(1)} %get-tuple-element.5), kind=kOutput, calls=%fused_computation.36 | convolution fusion | flops 684048384 | bytes 2949120 | tf_op jit(solution)/shard_map/qhpu,cpuw->chqw/dot_general | solution.py:150
  100.4 9.3 %all-gather.2.cloned.1.call-done = bf16[3,384,2,384]{1,3,2,0:T(8,128)(2,1)} async-done(((bf16[3,384,2,192]{1,3,2,0:T(8,128)(2,1)}), bf16[3,384,2,384]{1,3,2,0:T(8,128)(2,1)}) %all-gather.2.cloned.1.call-update) | async-done | bytes 1769488 | tf_op jit(solution)/shard_map/all_gather | solution.py:206
  109.6 2.0 %fusion.24 = bf16[3,384,192]{1,2,0:T(8,128)(2,1)S(1)} fusion(bf16[3,384,2,384]{1,3,2,0:T(8,128)(2,1)} %all-gather.2.cloned.1.call-done, bf16[1,384,192]{1,2,0:T(8,128)(2,1)S(1)} %get-tuple-element.20, bf16[1,384,192]{1,2,0:T(8,128)(2,1)S(1)} %get-tuple-element.18), kind=kOutput, calls=%fused_computation.39 | convolution fusion | flops 340770816 | bytes 2506752 | tf_op jit(solution)/shard_map/chqw,qwv->chv/dot_general | solution.py:207
  111.7 1.4 copy.35
  113.1 13.6 %all-to-all-start.1 = ((bf16[3,384,192]{2,0,1:T(4,128)(2,1)}), bf16[3,384,192]{2,0,1:T(4,128)(2,1)S(1)}, u32[]{:S(2)}, u32[]{:S(2)}) async-start(bf16[3,384,192]{2,0,1:T(4,128)(2,1)} %copy.35), calls=%async_computation.1 | async-start | bytes 1572864 | tf_op jit(solution)/shard_map/all_to_all | solution.py:211
  126.7 25.4 %all-to-all-done.1 = bf16[3,384,192]{2,0,1:T(4,128)(2,1)S(1)} async-done(((bf16[3,384,192]{2,0,1:T(4,128)(2,1)}), bf16[3,384,192]{2,0,1:T(4,128)(2,1)S(1)}, u32[]{:S(2)}, u32[]{:S(2)}) %all-to-all-start.1) | async-done | bytes 442400 | tf_op jit(solution)/shard_map/all_to_all | solution.py:211
  152.0 1.4 copy.36
  153.4 1.2 copy.37
  154.7 1.5 reshape.334
  156.2 3.4 %copy.38 = f32[128,3,3,192]{3,1,0,2:T(4,128)} copy(f32[128,3,3,192]{3,2,0,1:T(4,128)} %bitcast.136) | data formatting | bytes 1769472 | tf_op jit(solution)/shard_map/convert_element_type | solution.py:212
  159.5 1.8 reshape.333
  161.3 1.3 copy.39
  162.6 1.2 fusion.40
  163.8 0.3 constant_dynamic-slice_fusion.2
  164.1 1.9 %collective-permute-start.2 = (bf16[192,3,192]{0,2,1:T(8,128)(2,1)S(1)}, bf16[192,3,192]{0,2,1:T(8,128)(2,1)S(1)}, u32[]{:S(2)}, u32[]{:S(2)}) collective-permute-start(bf16[192,3,192]{0,2,1:T(8,128)(2,1)S(1)} %get-tuple-element.27), channel_id=1, source_target_pairs={{0,128},{128,0},{1,129},{129,1},{2,130},{130,2},{3,131},{131,3},{4... | collective-permute-start | bytes 663560 | tf_op jit(solution)/shard_map/ppermute | solution.py:215
  166.0 1.2 collective-permute-done.2
  167.3 0.2 maximum_select_fusion
  167.5 1.0 copy.40
  (30 shorter events, 0.3 us)
Async XLA Ops:
  6.5 7.8 %copy-start = (bf16[3,384,768]{2,1,0:T(8,128)(2,1)S(1)}, bf16[3,384,768]{2,1,0:T(8,128)(2,1)}, u32[]{:S(2)}) copy-start(bf16[3,384,768]{2,1,0:T(8,128)(2,1)} %param.9) | copy-start | bytes 5308420
  23.6 5.2 %collective-permute-start = (bf16[3,1,768]{2,1,0:T(2,128)(2,1)S(1)}, bf16[3,1,768]{2,1,0:T(2,128)(2,1)S(1)}, u32[]{:S(2)}, u32[]{:S(2)}) collective-permute-start(bf16[3,1,768]{2,1,0:T(2,128)(2,1)S(1)} %slice.72), channel_id=1, source_target_pairs={{0,128},{1,129},{2,130},{3,131},{4,132},{5,133},{6,134},{7,135},{8... | collective-permute-start | bytes 13832 | tf_op jit(solution)/shard_map/ppermute | solution.py:13
  28.9 9.4 %collective-permute-start.1 = (bf16[1,193,768]{2,1,0:T(8,128)(2,1)S(1)}, bf16[1,193,768]{2,1,0:T(8,128)(2,1)S(1)}, u32[]{:S(2)}, u32[]{:S(2)}) collective-permute-start(bf16[1,193,768]{2,1,0:T(8,128)(2,1)S(1)} %pad_maximum_fusion.8), channel_id=1, source_target_pairs={{0,1},{1,2},{2,3},{3,4},{4,5},{5,6},{6,7},{7,8},{8,9},{9,10},{10,1... | collective-permute-start | bytes 889352 | tf_op jit(solution)/shard_map/ppermute | solution.py:13
  36.4 2.2 %copy-start.3 = (bf16[2,2,192,384]{3,2,1,0:T(8,128)(2,1)S(1)}, bf16[2,2,192,384]{3,2,1,0:T(8,128)(2,1)}, u32[]{:S(2)}) copy-start(bf16[2,2,192,384]{3,2,1,0:T(8,128)(2,1)} %stack.125) | copy-start | bytes 1769476
  38.5 1.1 copy-start.1
  39.2 1.1 copy-start.2
  39.2 1.1 copy-start.8
  40.3 1.2 copy-start.9
  43.1 40.7 %all-to-all-start = ((bf16[384,3,192]{2,1,0:T(4,128)(2,1)}), bf16[384,3,192]{2,1,0:T(4,128)(2,1)S(1)}, u32[]{:S(2)}, u32[]{:S(2)}) async-start(bf16[384,3,192]{2,1,0:T(4,128)(2,1)} %copy.31), calls=%async_computation | async-start | bytes 1572864 | tf_op jit(solution)/shard_map/all_to_all | solution.py:183
  60.4 49.3 %all-gather.2.cloned.1.call-start = ((), (), s32[]{:S(2)}) async-start(), calls=%async_computation.2 | async-start | bytes 2654208 | tf_op jit(solution)/shard_map/all_gather | solution.py:206
  92.8 4.1 %copy-start.4 = (bf16[3,1,384,192]{2,3,1,0:T(8,128)(2,1)S(1)}, bf16[3,1,384,192]{2,3,1,0:T(8,128)(2,1)}, u32[]{:S(2)}) copy-start(bf16[3,1,384,192]{2,3,1,0:T(8,128)(2,1)} %copy.50) | copy-start | bytes 1327108
  92.8 4.1 %copy-start.5 = (bf16[3,1,384,192]{2,3,1,0:T(8,128)(2,1)S(1)}, bf16[3,1,384,192]{2,3,1,0:T(8,128)(2,1)}, u32[]{:S(2)}) copy-start(bf16[3,1,384,192]{2,3,1,0:T(8,128)(2,1)} %copy.51) | copy-start | bytes 1327108
  96.9 1.6 copy-start.6
  96.9 1.6 copy-start.7
  113.1 39.0 %all-to-all-start.1 = ((bf16[3,384,192]{2,0,1:T(4,128)(2,1)}), bf16[3,384,192]{2,0,1:T(4,128)(2,1)S(1)}, u32[]{:S(2)}, u32[]{:S(2)}) async-start(bf16[3,384,192]{2,0,1:T(4,128)(2,1)} %copy.35), calls=%async_computation.1 | async-start | bytes 1572864 | tf_op jit(solution)/shard_map/all_to_all | solution.py:211
  164.1 3.2 %collective-permute-start.2 = (bf16[192,3,192]{0,2,1:T(8,128)(2,1)S(1)}, bf16[192,3,192]{0,2,1:T(8,128)(2,1)S(1)}, u32[]{:S(2)}, u32[]{:S(2)}) collective-permute-start(bf16[192,3,192]{0,2,1:T(8,128)(2,1)S(1)} %get-tuple-element.27), channel_id=1, source_target_pairs={{0,128},{128,0},{1,129},{129,1},{2,130},{130,2},{3,131},{131,3},{4... | collective-permute-start | bytes 663560 | tf_op jit(solution)/shard_map/ppermute | solution.py:215
Sparse Core Ops, SparseCore 0:
  100.5 9.1 all-gather.1
where the time goes:
time: 176 us; the launch traced here: 175 us
  waiting for transfers between devices  44.7 us (25%)
  starting transfers between devices  38.1 us (22%)
  local copies, waits for them, and re-layouts  29.9 us (17%)
  matrix products  27 us (15%)
  other arithmetic  15.9 us (9%)
  between operations  13.7 us (8%)
  blocking collectives  6.01 us (3%)
    all_to_all x1, waiting for transfers between devices, local(): lax.all_to_all(filtered_fields, 'tile', split_axis=1, concat_axis=0, tile...  25.4 us
    all_to_all x1, starting transfers between devices, local(): lax.all_to_all(normed_half, 'tile', split_axis=0, concat_axis=1, tiled=True)  17.3 us
    all_to_all x1, starting transfers between devices, local(): lax.all_to_all(filtered_fields, 'tile', split_axis=1, concat_axis=0, tile...  13.6 us
    all_gather x1, waiting for transfers between devices, local(): back_rows = lax.all_gather(back_rows, 'section', axis=3, tiled=True)  9.27 us
    convert_element_type x5, local copies, waits for them, and re-layouts, local(): rows_back.astype(jnp.float32)  9.11 us
    all_to_all x1, waiting for transfers between devices, local(): lax.all_to_all(normed_half, 'tile', split_axis=0, concat_axis=1, tiled=True)  6.44 us
    all_gather x1, blocking collectives, local(): fields = lax.all_gather(fields, 'section', axis=2, tiled=True)  6.01 us
    ppermute x2, starting transfers between devices, from_behind(): return lax.ppermute(block, axis, route)  5.25 us
  transfers between devices with their start and end apart: 6, of which 6 were waited for; matrix products, arithmetic and copies ran while one was open for 14% of the time, Pallas kernels for 0%

commit v1 on v0

--- a/solution.py
+++ b/solution.py
@@ -181,7 +181,10 @@
     feature_half = down_conv(upper_rim, extended, down_weight, down_bias)
     normed_half = layer_norm(feature_half, norm_gain)
     fields = lax.all_to_all(normed_half, "tile", split_axis=0, concat_axis=1, tiled=True)
-    fields = lax.all_gather(fields, "section", axis=2, tiled=True)
+    n_dev = lax.axis_size("section")
+    pieces = jnp.stack([fields for _ in range(n_dev)])
+    pieces = lax.all_to_all(pieces, "section", split_axis=0, concat_axis=0)
+    fields = jnp.concatenate(pieces, axis=2)
     cos_h, sin_h = fourier_tables(full_rows)
     if full_rows == field_cols:
         cos_w, sin_w = (cos_h, sin_h)

time: 176 us -> 184 us (1.045)
  blocking collectives: 6.01 us -> 9.11 us
  local copies, waits for them, and re-layouts: 29.9 us -> 32.8 us
    all_to_all x0 -> x1, blocking collectives: none -> 9.11 us  [local(): pieces = lax.all_to_all(pieces, 'section', split_axis=0, concat_axis=0)]
    all_gather x1 -> x0, blocking collectives: 6.01 us -> none  [local(): fields = lax.all_gather(fields, 'section', axis=2, tiled=True)]
    another operation x0 -> x2, local copies, waits for them, and re-layouts: none -> 3.56 us  [local(): pieces = jnp.stack([fields for _ in range(n_dev)])]
    unnamed x22 -> x28, local copies, waits for them, and re-layouts: 4.61 us -> 4.63 us
  transfers between devices with their start and end apart: 6 -> 6, of which waited for: 6 -> 6; matrix products, arithmetic and copies ran while one was open for 14% -> 13% of each run, Pallas kernels for 0% -> 0%
where the time goes in v1:
time: 184 us; the launch traced here: 183 us
  waiting for transfers between devices  44.6 us (24%)
  starting transfers between devices  38.1 us (21%)
  local copies, waits for them, and re-layouts  32.8 us (18%)
  matrix products  26.9 us (15%)
  other arithmetic  17.5 us (10%)
  between operations  13.7 us (7%)
  blocking collectives  9.11 us (5%)
    all_to_all x1, waiting for transfers between devices, local(): lax.all_to_all(filtered_fields, 'tile', split_axis=1, concat_axis=0, tile...  25.4 us
    all_to_all x1, starting transfers between devices, local(): lax.all_to_all(normed_half, 'tile', split_axis=0, concat_axis=1, tiled=True)  17.3 us
    all_to_all x1, starting transfers between devices, local(): lax.all_to_all(filtered_fields, 'tile', split_axis=1, concat_axis=0, tile...  13.6 us
    all_gather x1, waiting for transfers between devices, local(): back_rows = lax.all_gather(back_rows, 'section', axis=3, tiled=True)  9.33 us
    convert_element_type x5, local copies, waits for them, and re-layouts, local(): rows_back.astype(jnp.float32)  9.12 us
    all_to_all x1, blocking collectives, local(): pieces = lax.all_to_all(pieces, 'section', split_axis=0, concat_axis=0)  9.11 us
    all_to_all x1, waiting for transfers between devices, local(): lax.all_to_all(normed_half, 'tile', split_axis=0, concat_axis=1, tiled=True)  6.38 us
    ppermute x2, starting transfers between devices, from_behind(): return lax.ppermute(block, axis, route)  5.25 us
  transfers between devices with their start and end apart: 6, of which 6 were waited for; matrix products, arithmetic and copies ran while one was open for 13% of the time, Pallas kernels for 0%

profile of v1, /device:TPU:1, one launch (start us, length us, event | category | flops | bytes accessed | tf_op | source)
XLA Modules:
  0.0 182.7 jit_solution(571520774312521849)
XLA Ops:
  6.6 0.8 tile.4
  7.4 0.1 add.318
  7.5 0.7 tile.5
  8.2 0.1 add.331
  8.3 2.5 %convolution_convert_fusion = bf16[1536,192]{0,1:T(8,128)(2,1)} fusion(bf16[384,192]{1,0:T(8,128)(2,1)} %bitcast.144, s32[1536]{0:T(1024)S(1)} %fusion.98), kind=kOutput, calls=%fused_computation.14 | convolution fusion | flops 227377152 | bytes 743424 | tf_op jit(solution)/shard_map/dot_general | solution.py:28
  10.8 3.5 %fusion.8 = bf16[768,1536,1]{1,0,2:T(8,128)(2,1)} fusion(s32[1536]{0:T(1024)S(1)} %get-tuple-element.41, s32[768]{0:T(1024)S(1)} %get-tuple-element.42, bf16[48,96]{1,0:T(8,128)(2,1)} %bitcast.145, s32[1536]{0:T(1024)S(1)} %get-tuple-element.40, s32[768]{0:T(1024)S(1)} %get-tuple-element.43), kind=kOutput, calls=%fused_computation.11 | convolution fusion | flops 237367296 | bytes 2386944 | tf_op jit(solution)/shard_map/dot_general | solution.py:35
  14.3 5.1 %fusion.7 = bf16[3,192,1536]{2,1,0:T(8,128)(2,1)} fusion(bf16[768,1536,1]{1,0,2:T(8,128)(2,1)} %fusion.8, f32[1536]{0:T(1024)S(1)} %add.318, bf16[3,384,768]{2,1,0:T(8,128)(2,1)S(1)} %copy-done, s32[]{:T(128)S(6)} %select_n.229), kind=kOutput, calls=%fused_computation.10 | convolution fusion | flops 1367801856 | bytes 5021700 | tf_op jit(solution)/shard_map/zji,if->zjf/dot_general | solution.py:85
  19.3 4.3 %fusion.17 = bf16[3,192,768]{2,1,0:T(8,128)(2,1)S(1)} fusion(bf16[3,192,1536]{2,1,0:T(8,128)(2,1)} %fusion.7, bf16[1536,192]{0,1:T(8,128)(2,1)} %convolution_convert_fusion, s32[768]{0:T(1024)S(1)} %get-tuple-element.45, s32[1536]{0:T(1024)S(1)} %fusion.91, f32[768]{0:T(1024)S(1)} %add.331, s32[768]{0:T(1024)S(1)} %get-tuple-element.44), kind=kOutput, calls=%fused_computation.23 | convolution fusion | flops 1820049408 | bytes 3259392 | tf_op jit(solution)/shard_map/zji,if->zjf/dot_general | solution.py:94
  23.6 1.3 collective-permute-start
  24.9 1.5 slice_bitcast_fusion.2
  26.5 0.9 pad_maximum_fusion.7
  27.5 0.9 pad_maximum_fusion.8
  28.4 0.4 collective-permute-done
  28.8 0.1 pad_maximum_fusion.9
  28.9 4.0 %collective-permute-start.1 = (bf16[1,193,768]{2,1,0:T(8,128)(2,1)S(1)}, bf16[1,193,768]{2,1,0:T(8,128)(2,1)S(1)}, u32[]{:S(2)}, u32[]{:S(2)}) collective-permute-start(bf16[1,193,768]{2,1,0:T(8,128)(2,1)S(1)} %pad_maximum_fusion.9), channel_id=1, source_target_pairs={{0,1},{1,2},{2,3},{3,4},{4,5},{5,6},{6,7},{7,8},{8,9},{9,10},{10,1... | collective-permute-start | bytes 889352 | tf_op jit(solution)/shard_map/ppermute | solution.py:13
  32.9 0.9 stack.124
  33.8 0.9 stack.132
  34.7 1.7 fusion.132
  36.4 1.9 %collective-permute-done.1 = bf16[1,193,768]{2,1,0:T(8,128)(2,1)S(1)} collective-permute-done((bf16[1,193,768]{2,1,0:T(8,128)(2,1)S(1)}, bf16[1,193,768]{2,1,0:T(8,128)(2,1)S(1)}, u32[]{:S(2)}, u32[]{:S(2)}) %collective-permute-start.1) | collective-permute-done | bytes 296480 | tf_op jit(solution)/shard_map/ppermute | solution.py:13
  38.3 0.2 maximum_maximum_fusion
  38.5 0.6 fusion.41
  39.2 0.4 copy-done.1
  39.6 0.6 convolution_add_fusion.1
  40.3 0.8 convert_reduce_fusion
  41.0 0.4 fusion.35
  41.4 0.2 fusion.34
  41.7 1.4 copy.34
  43.1 17.3 %all-to-all-start = ((bf16[384,3,192]{2,1,0:T(4,128)(2,1)}), bf16[384,3,192]{2,1,0:T(4,128)(2,1)S(1)}, u32[]{:S(2)}, u32[]{:S(2)}) async-start(bf16[384,3,192]{2,1,0:T(4,128)(2,1)} %copy.34), calls=%async_computation | async-start | bytes 1572864 | tf_op jit(solution)/shard_map/all_to_all | solution.py:183
  60.4 2.8 %constant_dynamic-slice_fusion = (bf16[3,1,384,192]{3,2,1,0:T(8,128)(2,1)}, bf16[3,1,384,192]{3,2,1,0:T(8,128)(2,1)}) fusion(bf16[3,2,384,384]{3,2,1,0:T(8,128)(2,1)} %param.17, s32[]{:T(128)S(6)} %select_n.229, s32[]{:T(128)S(6)} %add.349), kind=kLoop, calls=%fused_computation.233 | loop fusion | bytes 1769480 | tf_op jit(solution)/shard_map/slice | solution.py:141
  63.2 2.1 %copy.57 = bf16[3,1,384,192]{2,3,1,0:T(8,128)(2,1)} copy(bf16[3,1,384,192]{3,2,1,0:T(8,128)(2,1)} %get-tuple-element.7) | data formatting | bytes 884736
  65.3 2.1 %copy.58 = bf16[3,1,384,192]{2,3,1,0:T(8,128)(2,1)} copy(bf16[3,1,384,192]{3,2,1,0:T(8,128)(2,1)} %get-tuple-element.8) | data formatting | bytes 884736
  67.4 0.4 fusion.53
  67.7 1.6 fusion.76
  69.3 1.7 fusion.77
  71.0 2.3 %fusion.74 = bf16[384,1,384]{2,0,1:T(8,128)(2,1)S(1)} fusion(), kind=kLoop, calls=%fused_computation.132 | loop fusion | flops 1916928 | bytes 294912 | tf_op jit(solution)/shard_map/neg | solution.py:198
  73.4 2.6 %sine_convert_fusion = (bf16[384,1,384]{2,0,1:T(8,128)(2,1)S(1)}, bf16[384,1,384]{2,0,1:T(8,128)(2,1)S(1)}) fusion(), kind=kLoop, calls=%fused_computation.93 | loop fusion | flops 1622016 | bytes 589824 | tf_op jit(solution)/shard_map/convert_element_type | solution.py:20
  75.9 1.5 fusion.50
  77.4 6.4 %all-to-all-done = bf16[384,3,192]{2,1,0:T(4,128)(2,1)S(1)} async-done(((bf16[384,3,192]{2,1,0:T(4,128)(2,1)}), bf16[384,3,192]{2,1,0:T(4,128)(2,1)S(1)}, u32[]{:S(2)}, u32[]{:S(2)}) %all-to-all-start) | async-done | bytes 442400 | tf_op jit(solution)/shard_map/all_to_all | solution.py:183
  83.8 1.2 copy.36
  85.0 2.2 %stack.133 = bf16[1,3,384,192]{3,2,1,0:T(8,128)(2,1)} reshape(bf16[3,128,3,192]{3,2,1,0:T(4,128)(2,1)} %copy.36) | data formatting | bytes 884736 | tf_op jit(solution)/shard_map/stack | solution.py:185
  87.2 1.5 pad_maximum_fusion
  88.7 1.3 copy.37
  90.0 9.1 %all_to_all.29 = bf16[2,3,384,192]{2,3,1,0:T(8,128)(2,1)S(1)} all-to-all(bf16[2,3,384,192]{2,3,1,0:T(8,128)(2,1)} %copy.37), channel_id=1, replica_groups=mesh['section'=2,'tile'=128] {'section'}, dimensions={0} | all-to-all | bytes 1769472 | tf_op jit(solution)/shard_map/all_to_all | solution.py:186
  99.1 1.0 copy.38
  100.2 4.0 %fusion.21 = bf16[3,2,384,192]{2,3,1,0:T(8,128)(2,1)} fusion(bf16[1,384,2,384]{3,1,2,0:T(8,128)(2,1)} %get-tuple-element.29, bf16[1,384,2,384]{3,1,2,0:T(8,128)(2,1)} %get-tuple-element.22, bf16[3,384,384,1]{1,2,3,0:T(8,128)(2,1)} %bitcast.143, bf16[384,1,192]{0,2,1:T(8,128)(2,1)S(1)} %copy-done.10, bf16[384,1,192]{0,2,1:T(8,128)(2,1)S(1)} %copy-done.9), kind=kOutput, calls=%fused_computation.35 | convolution fusion | flops 1023049728 | bytes 3244032 | tf_op jit(solution)/shard_map/puqh,chqw->cpuw/dot_general | solution.py:136
  104.2 1.6 fusion.37
  105.8 1.8 fusion.22
  107.6 9.3 %all-gather.2.cloned.1.call-done = bf16[3,384,2,384]{1,3,2,0:T(8,128)(2,1)} async-done(((bf16[3,384,2,192]{1,3,2,0:T(8,128)(2,1)}), bf16[3,384,2,384]{1,3,2,0:T(8,128)(2,1)}) %all-gather.2.cloned.1.call-update) | async-done | bytes 1769488 | tf_op jit(solution)/shard_map/all_gather | solution.py:209
  117.0 2.0 %fusion.24 = bf16[3,384,192]{1,2,0:T(8,128)(2,1)S(1)} fusion(bf16[3,384,2,384]{1,3,2,0:T(8,128)(2,1)} %all-gather.2.cloned.1.call-done, bf16[1,384,192]{1,2,0:T(8,128)(2,1)S(1)} %copy-done.8, bf16[1,384,192]{1,2,0:T(8,128)(2,1)S(1)} %get-tuple-element.18), kind=kOutput, calls=%fused_computation.39 | convolution fusion | flops 340770816 | bytes 2506752 | tf_op jit(solution)/shard_map/chqw,qwv->chv/dot_general | solution.py:210
  119.0 1.4 copy.40
  120.4 13.6 %all-to-all-start.2 = ((bf16[3,384,192]{2,0,1:T(4,128)(2,1)}), bf16[3,384,192]{2,0,1:T(4,128)(2,1)S(1)}, u32[]{:S(2)}, u32[]{:S(2)}) async-start(bf16[3,384,192]{2,0,1:T(4,128)(2,1)} %copy.40), calls=%async_computation.2 | async-start | bytes 1572864 | tf_op jit(solution)/shard_map/all_to_all | solution.py:214
  134.0 25.4 %all-to-all-done.2 = bf16[3,384,192]{2,0,1:T(4,128)(2,1)S(1)} async-done(((bf16[3,384,192]{2,0,1:T(4,128)(2,1)}), bf16[3,384,192]{2,0,1:T(4,128)(2,1)S(1)}, u32[]{:S(2)}, u32[]{:S(2)}) %all-to-all-start.2) | async-done | bytes 442400 | tf_op jit(solution)/shard_map/all_to_all | solution.py:214
  159.4 1.4 copy.41
  160.8 1.2 copy.42
  162.0 1.5 reshape.343
  163.5 3.4 %copy.43 = f32[128,3,3,192]{3,1,0,2:T(4,128)} copy(f32[128,3,3,192]{3,2,0,1:T(4,128)} %bitcast.137) | data formatting | bytes 1769472 | tf_op jit(solution)/shard_map/convert_element_type | solution.py:215
  166.9 1.8 reshape.342
  168.6 1.3 copy.44
  169.9 1.2 fusion.40
  171.2 0.3 constant_dynamic-slice_fusion.2
  171.5 1.9 %collective-permute-start.2 = (bf16[192,3,192]{0,2,1:T(8,128)(2,1)S(1)}, bf16[192,3,192]{0,2,1:T(8,128)(2,1)S(1)}, u32[]{:S(2)}, u32[]{:S(2)}) collective-permute-start(bf16[192,3,192]{0,2,1:T(8,128)(2,1)S(1)} %get-tuple-element.27), channel_id=1, source_target_pairs={{0,128},{128,0},{1,129},{129,1},{2,130},{130,2},{3,131},{131,3},{4... | collective-permute-start | bytes 663560 | tf_op jit(solution)/shard_map/ppermute | solution.py:218
  173.4 1.2 collective-permute-done.2
  174.6 0.2 maximum_select_fusion
  174.8 1.0 copy.45
  (38 shorter events, 0.5 us)
Async XLA Ops:
  6.5 7.7 %copy-start = (bf16[3,384,768]{2,1,0:T(8,128)(2,1)S(1)}, bf16[3,384,768]{2,1,0:T(8,128)(2,1)}, u32[]{:S(2)}) copy-start(bf16[3,384,768]{2,1,0:T(8,128)(2,1)} %param.9) | copy-start | bytes 5308420
  23.6 5.2 %collective-permute-start = (bf16[3,1,768]{2,1,0:T(2,128)(2,1)S(1)}, bf16[3,1,768]{2,1,0:T(2,128)(2,1)S(1)}, u32[]{:S(2)}, u32[]{:S(2)}) collective-permute-start(bf16[3,1,768]{2,1,0:T(2,128)(2,1)S(1)} %slice.72), channel_id=1, source_target_pairs={{0,128},{1,129},{2,130},{3,131},{4,132},{5,133},{6,134},{7,135},{8... | collective-permute-start | bytes 13832 | tf_op jit(solution)/shard_map/ppermute | solution.py:13
  28.9 9.4 %collective-permute-start.1 = (bf16[1,193,768]{2,1,0:T(8,128)(2,1)S(1)}, bf16[1,193,768]{2,1,0:T(8,128)(2,1)S(1)}, u32[]{:S(2)}, u32[]{:S(2)}) collective-permute-start(bf16[1,193,768]{2,1,0:T(8,128)(2,1)S(1)} %pad_maximum_fusion.9), channel_id=1, source_target_pairs={{0,1},{1,2},{2,3},{3,4},{4,5},{5,6},{6,7},{7,8},{8,9},{9,10},{10,1... | collective-permute-start | bytes 889352 | tf_op jit(solution)/shard_map/ppermute | solution.py:13
  36.4 2.1 %copy-start.3 = (bf16[2,2,192,384]{3,2,1,0:T(8,128)(2,1)S(1)}, bf16[2,2,192,384]{3,2,1,0:T(8,128)(2,1)}, u32[]{:S(2)}) copy-start(bf16[2,2,192,384]{3,2,1,0:T(8,128)(2,1)} %stack.132) | copy-start | bytes 1769476
  38.5 1.1 copy-start.1
  39.1 1.1 copy-start.2
  39.2 1.1 copy-start.11
  40.3 1.2 copy-start.12
  43.1 40.7 %all-to-all-start = ((bf16[384,3,192]{2,1,0:T(4,128)(2,1)}), bf16[384,3,192]{2,1,0:T(4,128)(2,1)S(1)}, u32[]{:S(2)}, u32[]{:S(2)}) async-start(bf16[384,3,192]{2,1,0:T(4,128)(2,1)} %copy.34), calls=%async_computation | async-start | bytes 1572864 | tf_op jit(solution)/shard_map/all_to_all | solution.py:183
  60.4 56.6 %all-gather.2.cloned.1.call-start = ((), (), s32[]{:S(2)}) async-start(), calls=%async_computation.3 | async-start | bytes 2654208 | tf_op jit(solution)/shard_map/all_gather | solution.py:209
  90.0 10.1 %copy-start.9 = (bf16[384,1,192]{0,2,1:T(8,128)(2,1)S(1)}, bf16[384,1,192]{0,2,1:T(8,128)(2,1)}, u32[]{:S(2)}) copy-start(bf16[384,1,192]{0,2,1:T(8,128)(2,1)} %get-tuple-element.19) | copy-start | bytes 442372
  90.0 10.1 %copy-start.10 = (bf16[384,1,192]{0,2,1:T(8,128)(2,1)S(1)}, bf16[384,1,192]{0,2,1:T(8,128)(2,1)}, u32[]{:S(2)}) copy-start(bf16[384,1,192]{0,2,1:T(8,128)(2,1)} %get-tuple-element.21) | copy-start | bytes 442372
  100.2 4.0 %copy-start.4 = (bf16[3,1,384,192]{2,3,1,0:T(8,128)(2,1)S(1)}, bf16[3,1,384,192]{2,3,1,0:T(8,128)(2,1)}, u32[]{:S(2)}) copy-start(bf16[3,1,384,192]{2,3,1,0:T(8,128)(2,1)} %copy.57) | copy-start | bytes 1327108
  100.2 4.0 %copy-start.5 = (bf16[3,1,384,192]{2,3,1,0:T(8,128)(2,1)S(1)}, bf16[3,1,384,192]{2,3,1,0:T(8,128)(2,1)}, u32[]{:S(2)}) copy-start(bf16[3,1,384,192]{2,3,1,0:T(8,128)(2,1)} %copy.58) | copy-start | bytes 1327108
  104.2 1.6 copy-start.6
  104.2 1.6 copy-start.7
  105.8 11.2 %copy-start.8 = (bf16[1,384,192]{1,2,0:T(8,128)(2,1)S(1)}, bf16[1,384,192]{1,2,0:T(8,128)(2,1)}, u32[]{:S(2)}) copy-start(bf16[1,384,192]{1,2,0:T(8,128)(2,1)} %get-tuple-element.20) | copy-start | bytes 442372
  120.4 39.0 %all-to-all-start.2 = ((bf16[3,384,192]{2,0,1:T(4,128)(2,1)}), bf16[3,384,192]{2,0,1:T(4,128)(2,1)S(1)}, u32[]{:S(2)}, u32[]{:S(2)}) async-start(bf16[3,384,192]{2,0,1:T(4,128)(2,1)} %copy.40), calls=%async_computation.2 | async-start | bytes 1572864 | tf_op jit(solution)/shard_map/all_to_all | solution.py:214
  171.5 3.2 %collective-permute-start.2 = (bf16[192,3,192]{0,2,1:T(8,128)(2,1)S(1)}, bf16[192,3,192]{0,2,1:T(8,128)(2,1)S(1)}, u32[]{:S(2)}, u32[]{:S(2)}) collective-permute-start(bf16[192,3,192]{0,2,1:T(8,128)(2,1)S(1)} %get-tuple-element.27), channel_id=1, source_target_pairs={{0,128},{128,0},{1,129},{129,1},{2,130},{130,2},{3,131},{131,3},{4... | collective-permute-start | bytes 663560 | tf_op jit(solution)/shard_map/ppermute | solution.py:218
Sparse Core Ops, SparseCore 0:
  107.8 9.1 all-gather.1
